TPU v7x, 32 devices: a whole 2x2x4 slice. The times are simulated.
32 devices in a mesh: row: 8 (over z, y), col: 4 (over x, core).
Axes of the slice: x: 2, y: 2, z: 4, core: 2. Of those that a mesh axis runs over, the one named last changes fastest.
Arguments:
- sequence: bfloat16 [128, 1024], P('row'), may hold values from -6 to 6
- pair_state: bfloat16 [128, 128, 128], P('row', 'col'), may hold values from -6 to 6
- residue_mask: int32 [128], replicated, may hold values 0 or 1
- chain_index: int32 [128], replicated, may hold values from 0 to 3, never falling along the last dimension, each value on 1 to 64 neighbouring positions
- attention_in: bfloat16 [1024, 4, 1024], P(None, None, 'col'), may hold values from -0.1875 to 0.1875
- attention_out: bfloat16 [1024, 1024], P('col'), may hold values from -0.1875 to 0.1875
- bias_weight: bfloat16 [128, 32], replicated, may hold values from -40 to 40
- chain_bias: float32 [32], replicated, may hold values from -2 to 2
- outer_in: bfloat16 [1024, 128], replicated, may hold values from -0.1875 to 0.1875
- outer_out: bfloat16 [128, 128], replicated, may hold values from -0.5 to 0.5
- triangle_in: bfloat16 [128, 5, 128], replicated, may hold values from -0.5 to 0.5
- triangle_out: bfloat16 [128, 128], replicated, may hold values from -0.5 to 0.5
- transition_up: bfloat16 [128, 512], replicated, may hold values from -0.5 to 0.5
- transition_down: bfloat16 [512, 128], replicated, may hold values from -0.25 to 0.25
Outputs:
- sequence_out: bfloat16 [128, 1024], P('row')
- pair_out: bfloat16 [128, 128, 128], P('row', 'col')
Inputs may be any that keep to these rules, and one draw needn't show every extreme that they name: chain_index never falls along the residues; each chain holds at most 64 residues.
All inputs are finite; a program needn't handle non-finite values.
Results may differ from a plain program's by a relative error of at most 0.0095.
The roundings to bfloat16 on the way count: a program that leaves them out, or rounds other values in their place, can miss the bound.
Values may be sent and summed in bfloat16 or wider, within the bound.
A program may use at most 64 MiB of HBM per device.

v0:
```python
import math
import jax
import jax.numpy as jnp
from jax import lax
from jax.sharding import PartitionSpec as P


def layer_norm(values):
    center = values - jnp.mean(values, axis=-1, keepdims=True)
    spread = jnp.mean(center * center, axis=-1, keepdims=True)
    return center * lax.rsqrt(spread + 1e-05)


def per_device(
    sequence,
    pair_state,
    residue_mask,
    chain_index,
    attention_in,
    attention_out,
    bias_weight,
    chain_bias,
    outer_in,
    outer_out,
    triangle_in,
    triangle_out,
    transition_up,
    transition_down,
):
    rows_here, cols_here, channels = pair_state.shape
    length_all = residue_mask.shape[0]
    row_index = lax.axis_index("row")
    col_index = lax.axis_index("col")
    row_start = row_index * rows_here
    col_start = col_index * cols_here
    pair_wide = pair_state.astype(jnp.float32)
    normed_pair = layer_norm(pair_wide).astype(jnp.bfloat16)
    bias_tile = jnp.einsum(
        "ijc,ch->hij", normed_pair, bias_weight, preferred_element_type=jnp.float32
    )
    pair_bias = lax.all_to_all(bias_tile, "col", split_axis=0, concat_axis=2, tiled=True)
    heads_here = pair_bias.shape[0]
    normed_seq = layer_norm(sequence.astype(jnp.float32)).astype(jnp.bfloat16)
    projected = jnp.einsum(
        "id,dpe->ipe", normed_seq, attention_in, preferred_element_type=jnp.float32
    )
    query = projected[:, 0].astype(jnp.bfloat16)
    key_rows = projected[:, 1].astype(jnp.bfloat16)
    value_rows = projected[:, 2].astype(jnp.bfloat16)
    gate = jax.nn.sigmoid(projected[:, 3])
    keys_all, values_all = (
        lax.all_gather(key_rows, "row", axis=0, tiled=True),
        lax.all_gather(value_rows, "row", axis=0, tiled=True),
    )
    head_width = query.shape[1] // heads_here
    query_heads = query.reshape(rows_here, heads_here, head_width)
    key_heads = keys_all.reshape(length_all, heads_here, head_width)
    value_heads = values_all.reshape(length_all, heads_here, head_width)
    scale = 1.0 / math.sqrt(head_width)
    scores = (
        jnp.einsum("ihd,jhd->hij", query_heads, key_heads, preferred_element_type=jnp.float32)
        * scale
    )
    chain_rows = lax.dynamic_slice_in_dim(chain_index, row_start, rows_here, 0)
    same_chain = (chain_rows[:, None] == chain_index[None, :]).astype(jnp.float32)
    head_offset = lax.dynamic_slice_in_dim(chain_bias, col_index * heads_here, heads_here, 0)
    scores = scores + pair_bias + head_offset[:, None, None] * same_chain[None]
    positions = jnp.arange(length_all, dtype=jnp.int32)
    query_ids = row_start + jnp.arange(rows_here, dtype=jnp.int32)
    allowed = (residue_mask[None, :] == 1) | (query_ids[:, None] == positions[None, :])
    allowed = allowed[None]
    highest = jnp.max(jnp.where(allowed, scores, -jnp.inf), axis=-1, keepdims=True)
    raised = jnp.where(allowed, jnp.exp(scores - highest), 0.0)
    weights = (raised / jnp.sum(raised, axis=-1, keepdims=True)).astype(jnp.bfloat16)
    gathered = jnp.einsum(
        "hij,jhd->ihd", weights, value_heads, preferred_element_type=jnp.float32
    ).reshape(rows_here, -1)
    mixed = (gate * gathered).astype(jnp.bfloat16)
    head_terms = jnp.dot(mixed, attention_out, preferred_element_type=jnp.float32)
    update = lax.psum(head_terms, "col")
    sequence_out = (sequence.astype(jnp.float32) + update).astype(jnp.bfloat16)
    normed_out = layer_norm(sequence_out.astype(jnp.float32)).astype(jnp.bfloat16)
    outer_rows = jnp.dot(normed_out, outer_in, preferred_element_type=jnp.float32).astype(
        jnp.bfloat16
    )
    half_width = outer_rows.shape[1] // 2
    right_all = lax.all_gather(outer_rows[:, half_width:], "row", axis=0, tiled=True)
    right_side = lax.dynamic_slice_in_dim(right_all, col_start, cols_here, 0).astype(jnp.float32)
    left_side = outer_rows[:, :half_width].astype(jnp.float32)
    outer_feat = jnp.concatenate(
        [
            left_side[:, None, :] * right_side[None, :, :],
            left_side[:, None, :] - right_side[None, :, :],
        ],
        axis=-1,
    ).astype(jnp.bfloat16)
    pair_mid = pair_wide + jnp.dot(
        outer_feat.reshape(-1, 2 * half_width), outer_out, preferred_element_type=jnp.float32
    ).reshape(rows_here, cols_here, channels)
    normed_mid = layer_norm(pair_mid).astype(jnp.bfloat16)
    tri = jnp.dot(
        normed_mid.reshape(-1, channels),
        triangle_in.reshape(channels, -1),
        preferred_element_type=jnp.float32,
    ).reshape(rows_here, cols_here, 5, channels)
    live = residue_mask.astype(jnp.float32)
    row_live = lax.dynamic_slice_in_dim(live, row_start, rows_here, 0)
    col_live = lax.dynamic_slice_in_dim(live, col_start, cols_here, 0)
    pair_live = (row_live[:, None] * col_live[None, :])[:, :, None]
    left_op = (jax.nn.sigmoid(tri[:, :, 0]) * tri[:, :, 1] * pair_live).astype(jnp.bfloat16)
    right_op = (jax.nn.sigmoid(tri[:, :, 2]) * tri[:, :, 3] * pair_live).astype(jnp.bfloat16)
    out_gate = jax.nn.sigmoid(tri[:, :, 4])
    column_all = lax.all_gather(right_op, "row", axis=0, tiled=True)
    crossed = lax.psum_scatter(
        jnp.einsum("jkc,ikc->jic", column_all, left_op, preferred_element_type=jnp.float32),
        "col",
        scatter_dimension=0,
        tiled=True,
    )
    product = jnp.transpose(crossed, (1, 0, 2))
    normed_product = layer_norm(product).astype(jnp.bfloat16)
    projected_product = jnp.dot(
        normed_product.reshape(-1, channels), triangle_out, preferred_element_type=jnp.float32
    ).reshape(rows_here, cols_here, channels)
    pair_late = pair_mid + out_gate * projected_product
    normed_late = layer_norm(pair_late).astype(jnp.bfloat16)
    hidden = jax.nn.relu(
        jnp.dot(
            normed_late.reshape(-1, channels), transition_up, preferred_element_type=jnp.float32
        )
    ).astype(jnp.bfloat16)
    lowered = jnp.dot(hidden, transition_down, preferred_element_type=jnp.float32).reshape(
        rows_here, cols_here, channels
    )
    pair_out = (pair_late + lowered).astype(jnp.bfloat16)
    return (sequence_out, pair_out)


def solution(mesh):
    return jax.shard_map(
        per_device,
        mesh=mesh,
        in_specs=(
            P("row", None),
            P("row", "col", None),
            P(),
            P(),
            P(None, None, "col"),
            P("col", None),
            P(),
            P(),
            P(),
            P(),
            P(),
            P(),
            P(),
            P(),
        ),
        out_specs=(P("row", None), P("row", "col", None)),
        check_vma=False,
    )
```

profile of v0, /device:TPU:0, one launch (start us, length us, event | category | flops | bytes accessed | tf_op | source)
XLA Modules:
  0.0 257.6 jit_solution(43655018280628967)
XLA Ops:
  7.2 1.2 convert_reduce_fusion
  8.4 1.2 fusion.14
  9.6 1.2 convolution_bitcast_fusion.1
  11.0 0.8 reshape.259
  11.8 4.2 %all-to-all-start = ((f32[4,1,4096]{2,1,0:T(1,128)}), f32[4,1,4096]{2,1,0:T(1,128)S(1)}, u32[]{:S(2)}, u32[]{:S(2)}) async-start(f32[4,1,4096]{2,1,0:T(1,128)} %reshape.259), calls=%async_computation | async-start | bytes 131072 | tf_op jit(solution)/shard_map/all_to_all | solution.py:41
  16.0 0.7 convert_element_type.101
  16.7 0.7 broadcast_compare_fusion
  17.3 0.6 dynamic_slice.19
  17.9 0.7 dynamic_slice.18
  18.6 0.7 dynamic_slice.16
  19.3 0.9 convert_reduce_fusion.1
  20.2 0.9 fusion.50
  21.1 0.7 compare_convert_fusion
  21.9 1.9 fusion.92
  23.7 0.7 convert_element_type.87
  24.5 31.5 %all-gather.1 = bf16[128,1,256]{2,0,1:T(8,128)(2,1)S(1)} all-gather(bf16[16,1,256]{2,0,1:T(8,128)(2,1)S(1)} %get-tuple-element.7), channel_id=3, replica_groups=mesh['row'=8,'col'=4] {'row'}, dimensions={0}, use_global_device_ids=true | all-gather | bytes 73728 | tf_op jit(solution)/shard_map/all_gather | solution.py:52
  56.1 30.5 %all-gather = bf16[128,1,256]{2,0,1:T(8,128)(2,1)S(1)} all-gather(bf16[16,1,256]{2,0,1:T(8,128)(2,1)S(1)} %get-tuple-element.8), channel_id=2, replica_groups=mesh['row'=8,'col'=4] {'row'}, dimensions={0}, use_global_device_ids=true | all-gather | bytes 73728 | tf_op jit(solution)/shard_map/all_gather | solution.py:53
  86.6 0.7 copy.89
  87.4 0.5 broadcast.233
  88.0 0.8 reduce
  89.2 0.9 fusion.10
  90.4 1.1 convolution_bitcast_fusion.2
  91.6 1.5 fusion.74
  93.3 0.7 broadcast_multiply_fusion
  94.0 0.8 copy.95
  94.8 31.4 %all-reduce.2.cloned.1.call-done = f32[16,1024]{1,0:T(8,128)} async-done(((f32[16,1024]{1,0:T(8,128)}), f32[16,1024]{1,0:T(8,128)}) %all-reduce.2.cloned.1.call-update) | async-done | bytes 65552 | tf_op jit(solution)/shard_map/psum | solution.py:80
  126.2 1.0 convert_reduce_fusion.2
  127.4 0.2 convolution_convert_fusion
  127.7 30.7 %all_gather.14 = bf16[128,64]{1,0:T(8,128)(2,1)S(1)} all-gather(bf16[16,64]{1,0:T(8,128)(2,1)S(1)} %get-tuple-element.12), channel_id=1, replica_groups=mesh['row'=8,'col'=4] {'row'}, dimensions={0}, use_global_device_ids=true | all-gather | bytes 18432 | tf_op jit(solution)/shard_map/all_gather | solution.py:87
  158.4 1.1 fusion.94
  159.6 0.3 multiply_reduce_fusion.2
  159.8 0.4 copy-done.2
  160.3 1.3 fusion.32
  161.6 0.8 fusion.18
  162.5 1.2 copy.101
  163.7 39.1 %all-gather.4.cloned.1.call-done = bf16[128,32,128]{2,1,0:T(8,128)(2,1)} async-done(((bf16[16,32,128]{2,1,0:T(8,128)(2,1)}), bf16[128,32,128]{2,1,0:T(8,128)(2,1)}) %all-gather.4.cloned.1.call-update) | async-done | bytes 1048592 | tf_op jit(solution)/shard_map/all_gather | solution.py:113
  202.8 7.3 %copy.102 = bf16[128,32,128]{1,0,2:T(8,128)(2,1)} copy(bf16[128,32,128]{2,1,0:T(8,128)(2,1)} %all-gather.4.cloned.1.call-done) | data formatting | bytes 2097152 | tf_op jit(solution)/shard_map/all_gather | solution.py:113
  210.0 5.6 %convolution_bitcast_fusion = f32[128,16,128]{0,1,2:T(8,128)} fusion(bf16[16,32,128]{1,0,2:T(8,128)(2,1)} %copy.101, bf16[128,32,128]{1,0,2:T(8,128)(2,1)} %copy.102), kind=kOutput, calls=%fused_computation.4 | convolution fusion | flops 16777216 | bytes 2228224 | tf_op jit(solution)/shard_map/jkc,ikc->jic/dot_general | solution.py:115
  215.6 2.8 %copy.103 = f32[128,16,128]{2,1,0:T(8,128)} copy(f32[128,16,128]{0,1,2:T(8,128)} %convolution_bitcast_fusion) | data formatting | bytes 2097152 | tf_op jit(solution)/shard_map/jkc,ikc->jic/transpose | solution.py:115
  218.4 23.7 %reduce-scatter.2.cloned.1.call-done = f32[32,16,128]{2,1,0:T(8,128)} async-done(((f32[128,16,128]{2,1,0:T(8,128)}), f32[32,16,128]{2,1,0:T(8,128)}) %reduce-scatter.2.cloned.1.call-update) | async-done | bytes 262160 | tf_op jit(solution)/shard_map/reduce_scatter | solution.py:114
  242.1 1.1 bitcast_reduce_fusion
  243.4 1.2 multiply_reduce_fusion.1
  244.7 1.2 multiply_convert_fusion.1
  245.9 1.3 fusion.95
  247.2 0.3 multiply_reduce_fusion
  247.5 0.4 copy-done.1
  248.1 1.3 fusion.4
  249.4 1.6 add_convert_fusion
  (60 shorter events, 2.3 us)
Async XLA Ops:
  7.2 14.7 %copy-start = (bf16[1024,4,256]{2,1,0:T(4,128)(2,1)S(1)}, bf16[1024,4,256]{2,1,0:T(4,128)(2,1)}, u32[]{:S(2)}) copy-start(bf16[1024,4,256]{2,1,0:T(4,128)(2,1)} %param.18) | copy-start | bytes 6291460
  9.6 77.8 %copy-start.10 = (f32[32]{0:T(128)S(1)}, f32[32]{0:T(128)}, u32[]{:S(2)}) copy-start(f32[32]{0:T(128)} %param.21) | copy-start | bytes 388
  11.8 75.7 %all-to-all-start = ((f32[4,1,4096]{2,1,0:T(1,128)}), f32[4,1,4096]{2,1,0:T(1,128)S(1)}, u32[]{:S(2)}, u32[]{:S(2)}) async-start(f32[4,1,4096]{2,1,0:T(1,128)} %reshape.259), calls=%async_computation | async-start | bytes 131072 | tf_op jit(solution)/shard_map/all_to_all | solution.py:41
  16.0 110.2 %all-reduce.2.cloned.1.call-start = ((), (), s32[]{:S(2)}) async-start(), calls=%async_computation.2 | async-start | bytes 131072 | tf_op jit(solution)/shard_map/psum | solution.py:80
  21.9 69.8 %copy-start.5 = (bf16[256,1024]{1,0:T(8,128)(2,1)S(1)}, bf16[256,1024]{1,0:T(8,128)(2,1)}, u32[]{:S(2)}) copy-start(bf16[256,1024]{1,0:T(8,128)(2,1)} %param.19) | copy-start | bytes 1572868
  23.7 70.3 %copy-start.6 = (bf16[128,5,128]{2,0,1:T(8,128)(2,1)S(1)}, bf16[128,5,128]{2,0,1:T(8,128)(2,1)}, u32[]{:S(2)}) copy-start(bf16[128,5,128]{2,0,1:T(8,128)(2,1)} %param.24) | copy-start | bytes 491524
  23.7 102.5 %copy-start.4 = (bf16[16,1024]{1,0:T(8,128)(2,1)S(1)}, bf16[16,1024]{1,0:T(8,128)(2,1)}, u32[]{:S(2)}) copy-start(bf16[16,1024]{1,0:T(8,128)(2,1)} %param.14) | copy-start | bytes 98308
  87.4 71.1 %copy-start.3 = (bf16[16,32,128]{2,1,0:T(8,128)(2,1)S(1)}, bf16[16,32,128]{2,1,0:T(8,128)(2,1)}, u32[]{:S(2)}) copy-start(bf16[16,32,128]{2,1,0:T(8,128)(2,1)} %param.15) | copy-start | bytes 393220
  89.2 38.2 %copy-start.8 = (bf16[1024,128]{1,0:T(8,128)(2,1)S(1)}, bf16[1024,128]{1,0:T(8,128)(2,1)}, u32[]{:S(2)}) copy-start(bf16[1024,128]{1,0:T(8,128)(2,1)} %param.22) | copy-start | bytes 786436
  93.2 109.6 %all-gather.4.cloned.1.call-start = ((), (), s32[]{:S(2)}) async-start(), calls=%async_computation.3 | async-start | bytes 1179648 | tf_op jit(solution)/shard_map/all_gather | solution.py:113
  127.2 32.6 %copy-start.7 = (bf16[16,1024]{1,0:T(8,128)(2,1)}, bf16[16,1024]{1,0:T(8,128)(2,1)S(1)}, u32[]{:S(2)}) copy-start(bf16[16,1024]{1,0:T(8,128)(2,1)S(1)} %get-tuple-element.3) | copy-start | bytes 98308
  159.5 0.7 copy-start.2
  162.4 79.7 %reduce-scatter.2.cloned.1.call-start = ((), (), s32[]{:S(2)}) async-start(), calls=%async_computation.4 | async-start | bytes 1310720 | tf_op jit(solution)/shard_map/reduce_scatter | solution.py:114
  245.9 2.2 copy-start.9
  247.2 0.7 copy-start.1
Sparse Core Ops, SparseCore 0:
  93.3 32.8 all-reduce.1
  162.5 40.1 all-gather.3
  218.6 23.5 reduce-scatter.1
where the time goes:
time: 259 us; the launch traced here: 258 us
  waiting for transfers between devices  94.3 us (36%)
  blocking collectives  92.7 us (36%)
  local copies, waits for them, and re-layouts  18.8 us (7%)
  matrix products  17.5 us (7%)
  other arithmetic  16 us (6%)
  between operations  14 us (5%)
  starting transfers between devices  4.32 us (2%)
    all_gather x1, waiting for transfers between devices, per_device(): column_all = lax.all_gather(right_op, 'row', axis=0, tiled=True)  39.1 us
    all_gather x1, blocking collectives, per_device(): lax.all_gather(key_rows, 'row', axis=0, tiled=True)  31.5 us
    psum x1, waiting for transfers between devices, per_device(): update = lax.psum(head_terms, 'col')  31.4 us
    all_gather x1, blocking collectives, per_device(): lax.all_gather(outer_rows[:, half_width:], 'row', axis=0, tiled=True)  30.7 us
    all_gather x1, blocking collectives, per_device(): lax.all_gather(value_rows, 'row', axis=0, tiled=True)  30.5 us
    reduce_scatter x1, waiting for transfers between devices, per_device(): lax.psum_scatter(jnp.einsum('jkc,ikc->jic', column_all, left_op, preferre...  23.7 us
    all_gather x1, local copies, waits for them, and re-layouts, per_device(): column_all = lax.all_gather(right_op, 'row', axis=0, tiled=True)  7.25 us
    dot_general x1, matrix products, per_device(): jnp.einsum('jkc,ikc->jic', column_all, left_op, preferred_element_type=jn...  5.6 us
  transfers between devices with their start and end apart: 4, of which 3 were waited for; matrix products, arithmetic and copies ran while one was open for 5% of the time, Pallas kernels for 0%

commit v1 on v0

--- a/solution.py
+++ b/solution.py
@@ -77,7 +77,7 @@
     ).reshape(rows_here, -1)
     mixed = (gate * gathered).astype(jnp.bfloat16)
     head_terms = jnp.dot(mixed, attention_out, preferred_element_type=jnp.float32)
-    update = lax.psum(head_terms, "col")
+    update = jnp.sum(lax.all_gather(head_terms, "col"), axis=0)
     sequence_out = (sequence.astype(jnp.float32) + update).astype(jnp.bfloat16)
     normed_out = layer_norm(sequence_out.astype(jnp.float32)).astype(jnp.bfloat16)
     outer_rows = jnp.dot(normed_out, outer_in, preferred_element_type=jnp.float32).astype(

time: 259 us -> 233 us (0.90)
  waiting for transfers between devices: 94.3 us -> 63.8 us
  blocking collectives: 92.7 us -> 98.8 us
    psum x1 -> x0, waiting for transfers between devices: 31.4 us -> none  [per_device(): update = lax.psum(head_terms, 'col')]
    all_gather x0 -> x1, blocking collectives: none -> 6.17 us  [per_device(): update = jnp.sum(lax.all_gather(head_terms, 'col'), axis=0)]
  transfers between devices with their start and end apart: 4 -> 3, of which waited for: 3 -> 2; matrix products, arithmetic and copies ran while one was open for 5% -> 5% of each run, Pallas kernels for 0% -> 0%
where the time goes in v1:
time: 233 us; the launch traced here: 232 us
  blocking collectives  98.8 us (42%)
  waiting for transfers between devices  63.8 us (27%)
  local copies, waits for them, and re-layouts  17.7 us (8%)
  matrix products  17.1 us (7%)
  other arithmetic  15.8 us (7%)
  between operations  14.3 us (6%)
  starting transfers between devices  4.28 us (2%)
    all_gather x1, waiting for transfers between devices, per_device(): column_all = lax.all_gather(right_op, 'row', axis=0, tiled=True)  40.1 us
    all_gather x1, blocking collectives, per_device(): lax.all_gather(key_rows, 'row', axis=0, tiled=True)  31.5 us
    all_gather x1, blocking collectives, per_device(): lax.all_gather(outer_rows[:, half_width:], 'row', axis=0, tiled=True)  30.6 us
    all_gather x1, blocking collectives, per_device(): lax.all_gather(value_rows, 'row', axis=0, tiled=True)  30.5 us
    reduce_scatter x1, waiting for transfers between devices, per_device(): lax.psum_scatter(jnp.einsum('jkc,ikc->jic', column_all, left_op, preferre...  23.7 us
    all_gather x1, local copies, waits for them, and re-layouts, per_device(): column_all = lax.all_gather(right_op, 'row', axis=0, tiled=True)  7.25 us
    all_gather x1, blocking collectives, per_device(): update = jnp.sum(lax.all_gather(head_terms, 'col'), axis=0)  6.17 us
    dot_general x1, matrix products, per_device(): jnp.einsum('jkc,ikc->jic', column_all, left_op, preferred_element_type=jn...  5.6 us
  transfers between devices with their start and end apart: 3, of which 2 were waited for; matrix products, arithmetic and copies ran while one was open for 5% of the time, Pallas kernels for 0%

profile of v1, /device:TPU:0, one launch (start us, length us, event | category | flops | bytes accessed | tf_op | source)
XLA Modules:
  0.0 231.8 jit_solution(17554092579499673604)
XLA Ops:
  7.2 1.2 convert_reduce_fusion
  8.4 1.2 fusion.14
  9.6 1.3 convolution_bitcast_fusion.1
  11.0 0.8 reshape.260
  11.8 4.2 %all-to-all-start = ((f32[4,1,4096]{2,1,0:T(1,128)}), f32[4,1,4096]{2,1,0:T(1,128)S(1)}, u32[]{:S(2)}, u32[]{:S(2)}) async-start(f32[4,1,4096]{2,1,0:T(1,128)} %reshape.260), calls=%async_computation | async-start | bytes 131072 | tf_op jit(solution)/shard_map/all_to_all | solution.py:41
  16.1 0.7 convert_element_type.101
  16.7 0.7 broadcast_compare_fusion
  17.5 0.7 dynamic_slice.16
  18.2 0.9 convert_reduce_fusion.1
  19.1 0.9 fusion.50
  20.1 0.7 compare_convert_fusion
  20.8 1.8 fusion.92
  22.6 0.7 convert_element_type.87
  23.4 0.7 fusion.78
  24.1 31.5 %all-gather.1 = bf16[128,1,256]{2,0,1:T(8,128)(2,1)S(1)} all-gather(bf16[16,1,256]{2,0,1:T(8,128)(2,1)S(1)} %get-tuple-element.7), channel_id=3, replica_groups=mesh['row'=8,'col'=4] {'row'}, dimensions={0}, use_global_device_ids=true | all-gather | bytes 73728 | tf_op jit(solution)/shard_map/all_gather | solution.py:52
  55.7 30.5 %all-gather = bf16[128,1,256]{2,0,1:T(8,128)(2,1)S(1)} all-gather(bf16[16,1,256]{2,0,1:T(8,128)(2,1)S(1)} %get-tuple-element.8), channel_id=2, replica_groups=mesh['row'=8,'col'=4] {'row'}, dimensions={0}, use_global_device_ids=true | all-gather | bytes 73728 | tf_op jit(solution)/shard_map/all_gather | solution.py:53
  86.2 0.7 copy.89
  86.9 0.8 copy.95
  87.8 0.5 broadcast.233
  88.3 0.7 reduce
  89.5 0.9 fusion.10
  90.5 0.9 fusion.93
  91.4 1.1 convolution_bitcast_fusion.2
  92.7 0.9 fusion.74
  93.6 6.2 %all-gather.2 = f32[64,1024]{1,0:T(8,128)S(1)} all-gather(f32[16,1024]{1,0:T(8,128)S(1)} %fusion.74), channel_id=4, replica_groups=mesh['row'=8,'col'=4] {'col'}, dimensions={0}, use_global_device_ids=true | all-gather | bytes 327680 | tf_op jit(solution)/shard_map/all_gather | solution.py:80
  99.9 0.2 fusion.52
  100.1 1.2 convolution_convert_fusion
  101.3 30.6 %all_gather.22 = bf16[128,64]{1,0:T(8,128)(2,1)S(1)} all-gather(bf16[16,64]{1,0:T(8,128)(2,1)S(1)} %get-tuple-element.12), channel_id=1, replica_groups=mesh['row'=8,'col'=4] {'row'}, dimensions={0}, use_global_device_ids=true | all-gather | bytes 18432 | tf_op jit(solution)/shard_map/all_gather | solution.py:87
  132.0 0.3 fusion.94
  132.4 0.3 multiply_reduce_fusion.2
  132.7 0.4 copy-done.2
  133.1 1.3 fusion.32
  134.4 0.8 fusion.18
  135.3 1.2 copy.101
  136.5 40.1 %all-gather.5.cloned.1.call-done = bf16[128,32,128]{2,1,0:T(8,128)(2,1)} async-done(((bf16[16,32,128]{2,1,0:T(8,128)(2,1)}), bf16[128,32,128]{2,1,0:T(8,128)(2,1)}) %all-gather.5.cloned.1.call-update) | async-done | bytes 1048592 | tf_op jit(solution)/shard_map/all_gather | solution.py:113
  176.6 7.3 %copy.102 = bf16[128,32,128]{1,0,2:T(8,128)(2,1)} copy(bf16[128,32,128]{2,1,0:T(8,128)(2,1)} %all-gather.5.cloned.1.call-done) | data formatting | bytes 2097152 | tf_op jit(solution)/shard_map/all_gather | solution.py:113
  183.9 5.6 %convolution_bitcast_fusion = f32[128,16,128]{0,1,2:T(8,128)} fusion(bf16[16,32,128]{1,0,2:T(8,128)(2,1)} %copy.101, bf16[128,32,128]{1,0,2:T(8,128)(2,1)} %copy.102), kind=kOutput, calls=%fused_computation.4 | convolution fusion | flops 16777216 | bytes 2228224 | tf_op jit(solution)/shard_map/jkc,ikc->jic/dot_general | solution.py:115
  189.5 2.8 %copy.103 = f32[128,16,128]{2,1,0:T(8,128)} copy(f32[128,16,128]{0,1,2:T(8,128)} %convolution_bitcast_fusion) | data formatting | bytes 2097152 | tf_op jit(solution)/shard_map/jkc,ikc->jic/transpose | solution.py:115
  192.3 23.7 %reduce-scatter.2.cloned.1.call-done = f32[32,16,128]{2,1,0:T(8,128)} async-done(((f32[128,16,128]{2,1,0:T(8,128)}), f32[32,16,128]{2,1,0:T(8,128)}) %reduce-scatter.2.cloned.1.call-update) | async-done | bytes 262160 | tf_op jit(solution)/shard_map/reduce_scatter | solution.py:114
  216.0 1.1 bitcast_reduce_fusion
  217.2 1.2 multiply_reduce_fusion.1
  218.6 1.2 multiply_convert_fusion.1
  219.7 1.3 fusion.95
  221.1 0.3 multiply_reduce_fusion
  221.3 0.4 copy-done.1
  221.7 0.2 multiply_convert_fusion
  221.9 1.3 fusion.4
  223.3 1.6 add_convert_fusion
  (59 shorter events, 1.9 us)
Async XLA Ops:
  7.2 13.7 %copy-start = (bf16[1024,4,256]{2,1,0:T(4,128)(2,1)S(1)}, bf16[1024,4,256]{2,1,0:T(4,128)(2,1)}, u32[]{:S(2)}) copy-start(bf16[1024,4,256]{2,1,0:T(4,128)(2,1)} %param.18) | copy-start | bytes 6291460
  9.6 77.4 %copy-start.6 = (bf16[128,5,128]{2,0,1:T(8,128)(2,1)S(1)}, bf16[128,5,128]{2,0,1:T(8,128)(2,1)}, u32[]{:S(2)}) copy-start(bf16[128,5,128]{2,0,1:T(8,128)(2,1)} %param.24) | copy-start | bytes 491524
  10.8 76.9 %copy-start.10 = (f32[32]{0:T(128)S(1)}, f32[32]{0:T(128)}, u32[]{:S(2)}) copy-start(f32[32]{0:T(128)} %param.21) | copy-start | bytes 388
  11.8 76.0 %all-to-all-start = ((f32[4,1,4096]{2,1,0:T(1,128)}), f32[4,1,4096]{2,1,0:T(1,128)S(1)}, u32[]{:S(2)}, u32[]{:S(2)}) async-start(f32[4,1,4096]{2,1,0:T(1,128)} %reshape.260), calls=%async_computation | async-start | bytes 131072 | tf_op jit(solution)/shard_map/all_to_all | solution.py:41
  16.0 160.6 %all-gather.5.cloned.1.call-start = ((), (), s32[]{:S(2)}) async-start(), calls=%async_computation.2 | async-start | bytes 1179648 | tf_op jit(solution)/shard_map/all_gather | solution.py:113
  22.6 70.0 %copy-start.5 = (bf16[256,1024]{1,0:T(8,128)(2,1)S(1)}, bf16[256,1024]{1,0:T(8,128)(2,1)}, u32[]{:S(2)}) copy-start(bf16[256,1024]{1,0:T(8,128)(2,1)} %param.19) | copy-start | bytes 1572868
  55.5 44.2 %copy-start.4 = (bf16[16,1024]{1,0:T(8,128)(2,1)S(1)}, bf16[16,1024]{1,0:T(8,128)(2,1)}, u32[]{:S(2)}) copy-start(bf16[16,1024]{1,0:T(8,128)(2,1)} %param.14) | copy-start | bytes 98308
  89.1 43.0 %copy-start.3 = (bf16[16,32,128]{2,1,0:T(8,128)(2,1)S(1)}, bf16[16,32,128]{2,1,0:T(8,128)(2,1)}, u32[]{:S(2)}) copy-start(bf16[16,32,128]{2,1,0:T(8,128)(2,1)} %param.15) | copy-start | bytes 393220
  89.1 43.0 %copy-start.8 = (bf16[128,128]{1,0:T(8,128)(2,1)S(1)}, bf16[128,128]{1,0:T(8,128)(2,1)}, u32[]{:S(2)}) copy-start(bf16[128,128]{1,0:T(8,128)(2,1)} %param.23) | copy-start | bytes 98308
  99.9 32.8 %copy-start.7 = (bf16[16,1024]{1,0:T(8,128)(2,1)}, bf16[16,1024]{1,0:T(8,128)(2,1)S(1)}, u32[]{:S(2)}) copy-start(bf16[16,1024]{1,0:T(8,128)(2,1)S(1)} %get-tuple-element.3) | copy-start | bytes 98308
  132.4 0.7 copy-start.2
  135.3 80.7 %reduce-scatter.2.cloned.1.call-start = ((), (), s32[]{:S(2)}) async-start(), calls=%async_computation.3 | async-start | bytes 1310720 | tf_op jit(solution)/shard_map/reduce_scatter | solution.py:114
  219.7 2.2 copy-start.9
  221.0 0.7 copy-start.1
Sparse Core Ops, SparseCore 0:
  135.4 41.1 all-gather.4
  192.4 23.5 reduce-scatter.1
